TPU v7x, 128 devices: a whole 4x4x4 slice. The times are simulated.
128 devices in a mesh: row: 4 (over x), col: 16 (over z, y), depth: 2 (over core).
Axes of the slice: x: 4, y: 4, z: 4, core: 2. Of those that a mesh axis runs over, the one named last changes fastest.
Arguments:
- tokens: bfloat16 [2048, 8192], P('depth', 'col'), may hold values from -6 to 6
- weight: bfloat16 [8192, 14336], P('col', ('row', 'depth')), may hold values from -0.0625 to 0.0625
- block_mask: int32 [64, 112], replicated, may hold values 0 or 1
- cotangent: bfloat16 [2048, 14336], P('depth', 'row'), may hold values from -6 to 6
- example_ids: int32 [2048], replicated, may hold values from 0 to 3, as said below
Outputs:
- outputs: bfloat16 [2048, 14336], P('depth', 'row')
- grad_in: bfloat16 [2048, 8192], P('depth', 'col')
- grad_weight: bfloat16 [8192, 14336], P('col', ('row', 'depth'))
Inputs may be any that keep to these rules, and one draw needn't show every extreme that they name: `example_ids`: in the b-th aligned block of 1024 tokens (b from 0), the ids are 2 b for a first run of tokens and 2 b + 1 for the rest; each example has at least 128 tokens, and in every draw some example has exactly 896.
All inputs are finite; a program needn't handle non-finite values.
Results may differ from a plain program's by a relative error of at most 0.0052.
Values may be sent and summed in bfloat16 or wider, within the bound.
A program may use at most 128 MiB of HBM per device.

v0:
```python
import math
import jax
import jax.numpy as jnp
from jax import lax
from jax.sharding import PartitionSpec as P

D = 8192
FW = 14336
BLOCK = 128
TOK_DEV = 1024
EX_DEV = 2


def total_squares(partial_squares):
    return lax.psum(partial_squares, ("row", "col"))


def shards(tokens, weight, block_mask, cotangent, example_ids):
    tok_rows = tokens.shape[0]
    width_here = tokens.shape[1]
    hidden_here = cotangent.shape[1]
    col_at = lax.axis_index("col")
    row_at = lax.axis_index("row")
    depth_at = lax.axis_index("depth")
    tile_mask = lax.dynamic_slice(
        block_mask,
        (col_at * (width_here // BLOCK), row_at * (hidden_here // BLOCK)),
        (width_here // BLOCK, hidden_here // BLOCK),
    )
    keep = jnp.repeat(jnp.repeat(tile_mask > 0, BLOCK, axis=0), BLOCK, axis=1)
    zero_half = jnp.zeros((), jnp.bfloat16)
    ids_here = lax.dynamic_slice_in_dim(example_ids, depth_at * tok_rows, tok_rows)
    per_grads = []
    squares = []
    for slot in range(EX_DEV):
        chosen = ids_here == depth_at * EX_DEV + slot
        picked = jnp.where(chosen[:, None], cotangent, zero_half)
        product = lax.dot_general(
            tokens, picked, (((0,), (0,)), ((), ())), preferred_element_type=jnp.float32
        )
        product = jnp.where(keep, product, jnp.float32(0.0))
        per_grads.append(product)
        squares.append(jnp.sum(product * product))
    partial_squares = jnp.stack(squares)
    kept = keep
    out_part = jnp.dot(
        tokens,
        jnp.where(kept, lax.all_gather(weight, "depth", axis=1, tiled=True), zero_half),
        preferred_element_type=jnp.float32,
    )
    kept = keep
    masked_piece = jnp.where(kept, lax.all_gather(weight, "depth", axis=1, tiled=True), zero_half)
    back_part = lax.dot_general(
        cotangent, masked_piece, (((1,), (1,)), ((), ())), preferred_element_type=jnp.float32
    )
    out_sum = lax.psum(out_part, "col")
    back_sum = lax.psum(back_part, "row")
    all_squares = total_squares(partial_squares)
    out_final = out_sum.astype(jnp.bfloat16)
    back_final = back_sum.astype(jnp.bfloat16)
    bound = jnp.float32(0.5 * math.sqrt(D * FW * TOK_DEV))
    norms = jnp.sqrt(all_squares)
    factors = bound / jnp.maximum(norms, bound)
    examples_all = EX_DEV * lax.axis_size("depth")
    combined = jnp.zeros((width_here, hidden_here), jnp.float32)
    for slot in range(EX_DEV):
        combined = combined + factors[slot] * per_grads[slot]
    combined = combined / examples_all
    grad_sum = lax.psum_scatter(
        combined.astype(jnp.bfloat16), "depth", scatter_dimension=1, tiled=True
    )
    return (out_final, back_final, grad_sum)


def solution(mesh):
    placed = (P("depth", "col"), P("col", ("row", "depth")), P(), P("depth", "row"), P())
    return jax.shard_map(
        shards,
        mesh=mesh,
        in_specs=placed,
        out_specs=(P("depth", "row"), P("depth", "col"), P("col", ("row", "depth"))),
        check_vma=False,
    )
```

profile of v0, /device:TPU:0, one launch (start us, length us, event | category | flops | bytes accessed | tf_op | source)
XLA Modules:
  0.0 582.8 jit_solution(15162042323849801208)
XLA Ops:
  7.2 0.0 copy-start
  7.2 0.0 all-gather.2.cloned.1.call-start
  7.2 3.9 copy.9
  11.1 0.0 all-gather.2.cloned.1.call-update
  11.2 0.0 reduce-scatter.2.cloned.1.call-start
  11.2 0.8 dynamic-slice_compare_fusion.2
  12.0 0.1 copy.8
  12.1 0.1 broadcast_bitcast_fusion
  12.3 0.7 dynamic-slice_compare_fusion
  13.0 0.0 copy-done
  13.0 6.5 %fusion = f32[3584,512]{1,0:T(8,128)S(1)} fusion(bf16[1024,512]{1,0:T(8,128)(2,1)S(1)} %copy-done, bf16[1024,3584]{1,0:T(8,128)(2,1)} %param.8, pred[1024]{0:T(1024)(128)(4,1)S(1)} %get-tuple-element.8), kind=kOutput, calls=%fused_computation.6 | convolution fusion | flops 3761766400 | bytes 15729664 | tf_op jit(solution)/shard_map/dot_general | solution.py:38
  19.5 0.0 copy-start.1
  19.5 14.7 %multiply_reduce_fusion.1 = (f32[]{:T(128)}, f32[]{:T(128)}, f32[3584,512]{1,0:T(8,128)}) fusion(pred[512,28]{0,1:T(8,128)(4,1)S(1)} %bitcast.44, f32[3584,512]{1,0:T(8,128)S(1)} %fusion, bf16[1024,512]{1,0:T(8,128)(2,1)S(1)} %copy-done, bf16[1024,3584]{1,0:T(8,128)(2,1)} %param.8, pred[1024]{0:T(1024)(128)(4,1)S(1)} %get-tuple-element.9), kind=kOutput, calls=%fused_computation.8 | convolution fusion | flops 3772776448 | bytes 23084040 | tf_op jit(solution)/shard_map/dot_general | solution.py:38
  34.2 0.0 copy-done.1
  34.2 1.3 pad_maximum_fusion
  35.5 180.6 %psum.23 = f32[2]{0:T(128)S(1)} all-reduce(f32[2]{0:T(128)S(1)} %pad_maximum_fusion), channel_id=1, replica_groups=mesh['row'=4,'col'=16,'depth'=2] {'row','col'}, use_global_device_ids=true, to_apply=%region_4.5 | all-reduce | flops 2 | bytes 16 | tf_op jit(solution)/shard_map/psum | solution.py:15
  216.1 0.6 fusion.10
  216.7 9.2 %multiply_convert_fusion = bf16[512,3584]{0,1:T(8,128)(2,1)} fusion(f32[3584,512]{1,0:T(8,128)} %get-tuple-element.12, f32[3584,512]{1,0:T(8,128)} %copy-done.1, f32[]{:T(128)} %bitcast.8, f32[]{:T(128)} %bitcast.7, pred[512,28]{0,1:T(8,128)(4,1)S(1)} %bitcast.45), kind=kLoop, calls=%fused_computation.4 | loop fusion | flops 12845056 | bytes 18364424 | tf_op jit(solution)/shard_map/convert_element_type | solution.py:70
  225.9 0.0 reduce-scatter.2.cloned.1.call-update
  225.9 0.0 all-gather.2.cloned.1.call-done
  226.0 2.3 bitcast_select_fusion.2
  228.3 7.8 %convolution_bitcast_fusion.1 = f32[1024,512]{0,1:T(8,128)} fusion(bf16[512,3584]{0,1:T(8,128)(2,1)S(1)} %bitcast_select_fusion.2, bf16[1024,3584]{1,0:T(8,128)(2,1)} %param.8), kind=kOutput, calls=%fused_computation.15 | convolution fusion | flops 3758096384 | bytes 13107200 | tf_op jit(solution)/shard_map/dot_general | solution.py:53
  236.1 7.3 %convolution_bitcast_fusion = f32[1024,3584]{0,1:T(8,128)} fusion(bf16[512,3584]{0,1:T(8,128)(2,1)S(1)} %bitcast_select_fusion.2, bf16[1024,512]{1,0:T(8,128)(2,1)S(1)} %copy-done), kind=kOutput, calls=%fused_computation.3 | convolution fusion | flops 3758096384 | bytes 19398656 | tf_op jit(solution)/shard_map/dot_general | solution.py:46
  243.4 31.6 %all-reduce.2 = bf16[1024,512]{0,1:T(8,128)(2,1)S(1)} all-reduce(f32[1024,512]{0,1:T(8,128)} %convolution_bitcast_fusion.1), channel_id=1, replica_groups=mesh['row'=4,'col'=16,'depth'=2] {'row'}, use_global_device_ids=true, to_apply=%region_1.2 | all-reduce | flops 524288 | bytes 3145728 | tf_op jit(solution)/shard_map/psum | solution.py:57
  275.0 1.3 copy.11
  276.4 285.8 %all-reduce.3 = bf16[1024,3584]{0,1:T(8,128)(2,1)} all-reduce(f32[1024,3584]{0,1:T(8,128)} %convolution_bitcast_fusion), channel_id=1, replica_groups=mesh['row'=4,'col'=16,'depth'=2] {'col'}, use_global_device_ids=true, to_apply=%region_0.1 | all-reduce | flops 3670016 | bytes 22020096 | tf_op jit(solution)/shard_map/psum | solution.py:56
  562.2 9.9 %copy.10 = bf16[1024,3584]{1,0:T(8,128)(2,1)} copy(bf16[1024,3584]{0,1:T(8,128)(2,1)} %all-reduce.3) | data formatting | bytes 14680064
  572.1 0.0 reduce-scatter.2.cloned.1.call-done
  572.1 3.8 copy.12
  (3 shorter events, 0.0 us)
Async XLA Ops:
  7.2 5.8 copy-start
  7.2 218.8 %all-gather.2.cloned.1.call-start = ((), (), s32[]{:S(2)}) async-start(), calls=%async_computation.1 | async-start | bytes 5505024 | tf_op jit(solution)/shard_map/all_gather | solution.py:48
  11.2 561.0 %reduce-scatter.2.cloned.1.call-start = ((), (), s32[]{:S(2)}) async-start(), calls=%async_computation.2 | async-start | bytes 5505024 | tf_op jit(solution)/shard_map/reduce_scatter | solution.py:69
  19.5 14.8 %copy-start.1 = (f32[3584,512]{1,0:T(8,128)}, f32[3584,512]{1,0:T(8,128)S(1)}, u32[]{:S(2)}) copy-start(f32[3584,512]{1,0:T(8,128)S(1)} %fusion) | copy-start | bytes 22020100
Sparse Core Ops, SparseCore 0:
  11.3 18.0 all-gather.1
  226.0 8.0 reduce-scatter.1
where the time goes:
time: 583 us
  blocking collectives  498 us (85%)
  matrix products  36.3 us (6%)
  local copies, waits for them, and re-layouts  19.8 us (3%)
  other arithmetic  14.3 us (2%)
  between operations  14.1 us (2%)
    psum x1, blocking collectives, shards(): out_sum = lax.psum(out_part, 'col')  286 us
    psum x1, blocking collectives, total_squares(): return lax.psum(partial_squares, ('row', 'col'))  181 us
    psum x1, blocking collectives, shards(): back_sum = lax.psum(back_part, 'row')  31.6 us
    dot_general x2, matrix products, shards(): lax.dot_general(tokens, picked, (((0,), (0,)), ((), ())), preferred_eleme...  21.2 us
    unnamed x11, local copies, waits for them, and re-layouts  19.1 us
  transfers between devices with their start and end apart: 2, of which 0 were waited for; matrix products, arithmetic and copies ran while one was open for 11% of the time, Pallas kernels for 0%

commit v1 on v0

--- a/solution.py
+++ b/solution.py
@@ -53,7 +53,9 @@
     back_part = lax.dot_general(
         cotangent, masked_piece, (((1,), (1,)), ((), ())), preferred_element_type=jnp.float32
     )
-    out_sum = lax.psum(out_part, "col")
+    out_sum = out_part
+    for hop in (1, 2, 4, 8):
+        out_sum = out_sum + lax.ppermute(out_sum, "col", [(dev, dev ^ hop) for dev in range(16)])
     back_sum = lax.psum(back_part, "row")
     all_squares = total_squares(partial_squares)
     out_final = out_sum.astype(jnp.bfloat16)

time: 583 us -> 1360 us (2.33)
  waiting for transfers between devices: 0.06 us -> 1020 us
  blocking collectives: 498 us -> 211 us
  other arithmetic: 14.3 us -> 48.5 us
    ppermute x0 -> x4, waiting for transfers between devices: none -> 1000 us  [shards(): lax.ppermute(out_sum, 'col', [(dev, dev ^ hop) for dev in range(16)])]
    psum x1 -> x0, blocking collectives: 286 us -> none  [shards(): out_sum = lax.psum(out_part, 'col')]
    add x0 -> x3, other arithmetic: none -> 21.4 us  [shards(): out_sum + lax.ppermute(out_sum, 'col', [(dev, dev ^ hop) for dev in range...]
    all_gather x1, waiting for transfers between devices: 0.02 us -> 17.1 us  [shards(): lax.all_gather(weight, 'depth', axis=1, tiled=True)]
  transfers between devices with their start and end apart: 2 -> 6, of which waited for: 0 -> 5; matrix products, arithmetic and copies ran while one was open for 11% -> 4% of each run, Pallas kernels for 0% -> 0%
where the time goes in v1:
time: 1360 us
  waiting for transfers between devices  1020 us (75%)
  blocking collectives  211 us (16%)
  other arithmetic  48.5 us (4%)
  matrix products  35.7 us (3%)
  local copies, waits for them, and re-layouts  19.8 us (1%)
  between operations  14.2 us (1%)
    ppermute x4, waiting for transfers between devices, shards(): lax.ppermute(out_sum, 'col', [(dev, dev ^ hop) for dev in range(16)])  1000 us
    psum x1, blocking collectives, total_squares(): return lax.psum(partial_squares, ('row', 'col'))  179 us
    psum x1, blocking collectives, shards(): back_sum = lax.psum(back_part, 'row')  31.6 us
  transfers between devices with their start and end apart: 6, of which 5 were waited for; matrix products, arithmetic and copies ran while one was open for 4% of the time, Pallas kernels for 0%

profile of v1, /device:TPU:0, one launch (start us, length us, event | category | flops | bytes accessed | tf_op | source)
XLA Modules:
  0.0 1359.7 jit_solution(6343700674889137479)
XLA Ops:
  7.2 0.0 copy-start
  7.2 0.0 all-gather.2.cloned.1.call-start
  7.2 3.9 copy.9
  11.1 0.0 all-gather.2.cloned.1.call-update
  11.2 0.0 reduce-scatter.2.cloned.1.call-start
  11.2 0.8 dynamic-slice_compare_fusion.2
  12.0 0.1 copy.8
  12.1 0.1 broadcast_bitcast_fusion
  12.3 17.1 %all-gather.2.cloned.1.call-done = bf16[512,3584]{0,1:T(8,128)(2,1)} async-done(((bf16[512,1792]{0,1:T(8,128)(2,1)}), bf16[512,3584]{0,1:T(8,128)(2,1)}) %all-gather.2.cloned.1.call-update) | async-done | bytes 3670032 | tf_op jit(solution)/shard_map/all_gather | solution.py:48
  29.4 2.3 bitcast_select_fusion.2
  31.7 0.0 copy-done
  31.7 0.0 copy-start.2
  31.7 4.3 convolution_bitcast_fusion
  36.0 0.0 copy-done.2
  36.1 1.7 collective-permute-start
  37.7 316.0 %collective-permute-done = f32[1024,3584]{0,1:T(8,128)} collective-permute-done((f32[1024,3584]{0,1:T(8,128)S(1)}, f32[1024,3584]{0,1:T(8,128)}, u32[]{:S(2)}, u32[]{:S(2)}) %collective-permute-start) | collective-permute-done | bytes 14680096 | tf_op jit(solution)/shard_map/ppermute | solution.py:58
  353.7 7.2 add.35
  360.9 3.2 collective-permute-start.1
  364.1 315.1 %collective-permute-done.1 = f32[1024,3584]{0,1:T(8,128)} collective-permute-done((f32[1024,3584]{0,1:T(8,128)S(1)}, f32[1024,3584]{0,1:T(8,128)}, u32[]{:S(2)}, u32[]{:S(2)}) %collective-permute-start.1) | collective-permute-done | bytes 14680096 | tf_op jit(solution)/shard_map/ppermute | solution.py:58
  679.2 7.2 add.36
  686.4 0.0 copy-start.3
  686.4 1.7 collective-permute-start.2
  688.1 314.1 %collective-permute-done.2 = f32[1024,3584]{0,1:T(8,128)S(1)} collective-permute-done((f32[1024,3584]{0,1:T(8,128)S(1)}, f32[1024,3584]{0,1:T(8,128)S(1)}, u32[]{:S(2)}, u32[]{:S(2)}) %collective-permute-start.2) | collective-permute-done | bytes 14680096 | tf_op jit(solution)/shard_map/ppermute | solution.py:58
  1002.2 7.0 add.37
  1009.3 3.2 collective-permute-start.3
  1012.5 0.0 copy-done.3
  1012.5 6.5 fusion
  1019.0 0.0 copy-start.1
  1019.0 14.2 %multiply_reduce_fusion.1 = (f32[]{:T(128)}, f32[]{:T(128)}, f32[3584,512]{1,0:T(8,128)}) fusion(pred[512,28]{0,1:T(8,128)(4,1)S(1)} %bitcast.45, f32[3584,512]{1,0:T(8,128)S(1)} %fusion, bf16[1024,512]{1,0:T(8,128)(2,1)S(1)} %copy-done, bf16[1024,3584]{1,0:T(8,128)(2,1)} %param.8, pred[1024]{0:T(1024)(128)(4,1)S(1)} %get-tuple-element.9), kind=kOutput, calls=%fused_computation.9 | convolution fusion | flops 3772776448 | bytes 23084040 | tf_op jit(solution)/shard_map/dot_general | solution.py:38
  1033.2 0.0 copy-done.1
  1033.2 1.4 pad_maximum_fusion
  1034.6 179.4 %psum.15 = f32[2]{0:T(128)S(1)} all-reduce(f32[2]{0:T(128)S(1)} %pad_maximum_fusion), channel_id=1, replica_groups=mesh['row'=4,'col'=16,'depth'=2] {'row','col'}, use_global_device_ids=true, to_apply=%region_3.4 | all-reduce | flops 2 | bytes 16 | tf_op jit(solution)/shard_map/psum | solution.py:15
  1213.9 0.6 fusion.10
  1214.5 9.3 multiply_convert_fusion
  1223.9 0.0 reduce-scatter.2.cloned.1.call-update
  1223.9 10.7 convolution_bitcast_fusion.1
  1234.6 31.6 %all-reduce.1 = bf16[1024,512]{0,1:T(8,128)(2,1)S(1)} all-reduce(f32[1024,512]{0,1:T(8,128)} %convolution_bitcast_fusion.1), channel_id=1, replica_groups=mesh['row'=4,'col'=16,'depth'=2] {'row'}, use_global_device_ids=true, to_apply=%region_0.1 | all-reduce | flops 524288 | bytes 3145728 | tf_op jit(solution)/shard_map/psum | solution.py:59
  1266.3 1.3 copy.11
  1267.6 0.0 reduce-scatter.2.cloned.1.call-done
  1267.6 3.8 copy.12
  1271.4 58.1 %collective-permute-done.3 = f32[1024,3584]{0,1:T(8,128)} collective-permute-done((f32[1024,3584]{0,1:T(8,128)}, f32[1024,3584]{0,1:T(8,128)}, u32[]{:S(2)}, u32[]{:S(2)}) %collective-permute-start.3) | collective-permute-done | bytes 14680096 | tf_op jit(solution)/shard_map/ppermute | solution.py:58
  1329.5 13.4 add_convert_fusion
  1342.9 9.9 copy.10
  (4 shorter events, 0.1 us)
Async XLA Ops:
  7.2 24.5 %copy-start = (bf16[1024,512]{1,0:T(8,128)(2,1)S(1)}, bf16[1024,512]{1,0:T(8,128)(2,1)}, u32[]{:S(2)}) copy-start(bf16[1024,512]{1,0:T(8,128)(2,1)} %param.5) | copy-start | bytes 3145732
  7.2 22.2 %all-gather.2.cloned.1.call-start = ((), (), s32[]{:S(2)}) async-start(), calls=%async_computation.1 | async-start | bytes 5505024 | tf_op jit(solution)/shard_map/all_gather | solution.py:48
  11.2 1256.4 %reduce-scatter.2.cloned.1.call-start = ((), (), s32[]{:S(2)}) async-start(), calls=%async_computation.2 | async-start | bytes 5505024 | tf_op jit(solution)/shard_map/reduce_scatter | solution.py:71
  31.7 4.3 copy-start.2
  36.1 317.7 %collective-permute-start = (f32[1024,3584]{0,1:T(8,128)S(1)}, f32[1024,3584]{0,1:T(8,128)}, u32[]{:S(2)}, u32[]{:S(2)}) collective-permute-start(f32[1024,3584]{0,1:T(8,128)S(1)} %convolution_bitcast_fusion), channel_id=1, source_target_pairs={{0,2},{2,0},{4,6},{6,4},{8,10},{10,8},{12,14},{14,12},{16,18},{18,... | collective-permute-start | bytes 44040200 | tf_op jit(solution)/shard_map/ppermute | solution.py:58
  360.9 318.3 %collective-permute-start.1 = (f32[1024,3584]{0,1:T(8,128)S(1)}, f32[1024,3584]{0,1:T(8,128)}, u32[]{:S(2)}, u32[]{:S(2)}) collective-permute-start(f32[1024,3584]{0,1:T(8,128)S(1)} %add.35), channel_id=1, source_target_pairs={{0,4},{2,6},{4,0},{6,2},{8,12},{10,14},{12,8},{14,10},{16,20},{18,... | collective-permute-start | bytes 44040200 | tf_op jit(solution)/shard_map/ppermute | solution.py:58
  686.4 326.1 %copy-start.3 = (s32[2048]{0:T(1024)S(1)}, s32[2048]{0:T(1024)}, u32[]{:S(2)}) copy-start(s32[2048]{0:T(1024)} %param.9) | copy-start | bytes 24580
  686.4 315.8 %collective-permute-start.2 = (f32[1024,3584]{0,1:T(8,128)S(1)}, f32[1024,3584]{0,1:T(8,128)S(1)}, u32[]{:S(2)}, u32[]{:S(2)}) collective-permute-start(f32[1024,3584]{0,1:T(8,128)S(1)} %add.36), channel_id=1, source_target_pairs={{0,8},{2,10},{4,12},{6,14},{8,0},{10,2},{12,4},{14,6},{16,24},{18,... | collective-permute-start | bytes 44040200 | tf_op jit(solution)/shard_map/ppermute | solution.py:58
  1009.3 320.3 %collective-permute-start.3 = (f32[1024,3584]{0,1:T(8,128)}, f32[1024,3584]{0,1:T(8,128)}, u32[]{:S(2)}, u32[]{:S(2)}) collective-permute-start(f32[1024,3584]{0,1:T(8,128)} %add.37), channel_id=1, source_target_pairs={{0,16},{2,18},{4,20},{6,22},{8,24},{10,26},{12,28},{14,30},{16,0},... | collective-permute-start | bytes 44040200 | tf_op jit(solution)/shard_map/ppermute | solution.py:58
  1019.0 14.2 %copy-start.1 = (f32[3584,512]{1,0:T(8,128)}, f32[3584,512]{1,0:T(8,128)S(1)}, u32[]{:S(2)}) copy-start(f32[3584,512]{1,0:T(8,128)S(1)} %fusion) | copy-start | bytes 22020100
Sparse Core Ops, SparseCore 0:
  11.3 18.0 all-gather.1
  1224.0 8.0 reduce-scatter.1
